TPU v7x, 256 devices: a whole 4x4x8 slice. The times are simulated.
256 devices in a mesh: row: 8 (over z_hi, core), col: 32 (over x, z_lo, y).
Axes of the slice: x: 4, y: 4, z: 8 (z_hi: 4, z_lo: 2; z = z_hi * 2 + z_lo), core: 2. Of those that a mesh axis runs over, the one named last changes fastest.
Arguments:
- features: bfloat16 [131072, 128], P(('row', 'col')), may hold values from -6 to 6
- weight: bfloat16 [128, 128], replicated, may hold values from -0.5 to 0.5
- bias: float32 [128], replicated, may hold values from -3 to 3
- cotangent: bfloat16 [131072, 128], P(('row', 'col')), may hold values from -6 to 6
- block_count: int32 [8, 32], P('row', 'col'), may hold values from 64 to 512
- block_rows: int32 [8, 32, 512], P('row', 'col'), may hold values from 0 to 127
- block_cols: int32 [8, 32, 512], P('row', 'col'), may hold values from 0 to 31
- edge_offsets: int32 [8, 32, 512, 128], P('row', 'col'), may hold values from 0 to 16383, as said below
- edge_weight: bfloat16 [8, 32, 512, 128], P('row', 'col'), may hold values from 0.0099487305 to 0.099609375
Outputs:
- output: bfloat16 [131072, 128], P(('row', 'col'))
- grad_features: bfloat16 [131072, 128], P(('row', 'col'))
- grad_weight: float32 [128, 128], replicated
- grad_bias: float32 [128], replicated
Inputs may be any that keep to these rules, and one draw needn't show every extreme that they name: `edge_offsets`: the offsets within one slot are distinct.
All inputs are finite; a program needn't handle non-finite values.
Results may differ from a plain program's by a relative error of at most 0.013.
The roundings to bfloat16 on the way count: a program that leaves them out, or rounds other values in their place, can miss the bound.
Values may be sent and summed in bfloat16 or wider, within the bound.
A program may use at most 128 MiB of HBM per device.

v0:
```python
import jax
import jax.numpy as jnp
from jax import lax
from jax.sharding import PartitionSpec as P


def shards(
    features,
    weight,
    bias,
    cotangent,
    block_count,
    block_rows,
    block_cols,
    edge_offsets,
    edge_weight,
):
    node_dev, width = features.shape
    n_row = lax.axis_size("row")
    n_col = lax.axis_size("col")
    slots = block_rows.shape[2]
    batch = min(64, slots)
    count = block_count[0, 0]
    turns = (count + batch - 1) // batch
    brow = block_rows[0, 0]
    bcol = block_cols[0, 0]
    offsets = edge_offsets[0, 0]
    weights = edge_weight[0, 0]
    lanes = jnp.arange(batch, dtype=jnp.int32)
    within = jnp.arange(128, dtype=jnp.int32)
    row_blocks = node_dev * n_col // 128
    col_blocks = node_dev * n_row // 128
    row_ids = jnp.arange(row_blocks, dtype=jnp.int32)
    col_ids = jnp.arange(col_blocks, dtype=jnp.int32)
    projected = jnp.dot(features, weight, preferred_element_type=jnp.float32).astype(jnp.bfloat16)
    panel = lax.all_gather(projected, "row", axis=0, tiled=True).reshape(-1, 128, width)

    def forward_step(i, carry):
        stored, totals = carry
        start = i * batch
        offs = lax.dynamic_slice_in_dim(offsets, start, batch, 0)
        vals = lax.dynamic_slice_in_dim(weights, start, batch, 0).astype(jnp.float32)
        vals = jnp.where((start + lanes < count)[:, None], vals, 0.0)
        left = jnp.where((offs // 128)[:, :, None] == within, vals[:, :, None], 0.0).astype(
            jnp.bfloat16
        )
        right = ((offs % 128)[:, :, None] == within).astype(jnp.bfloat16)
        dense = jnp.einsum("bei,bej->bij", left, right, preferred_element_type=jnp.float32).astype(
            jnp.bfloat16
        )
        stored = lax.dynamic_update_slice_in_dim(stored, dense, start, 0)
        rows_here = lax.dynamic_slice_in_dim(brow, start, batch, 0)
        cols_here = lax.dynamic_slice_in_dim(bcol, start, batch, 0)
        product = jnp.einsum(
            "bij,bjf->bif", dense, panel[cols_here], preferred_element_type=jnp.float32
        )
        select = (rows_here[:, None] == row_ids).astype(jnp.float32)
        added = jnp.einsum(
            "br,bif->rif",
            select,
            product,
            precision=lax.Precision.HIGHEST,
            preferred_element_type=jnp.float32,
        )
        return (stored, totals + added)

    stored0 = jnp.zeros((slots, 128, 128), jnp.bfloat16)
    totals0 = jnp.zeros((row_blocks, 128, width), jnp.float32)
    stored, totals = lax.fori_loop(0, turns, forward_step, (stored0, totals0))
    totals = totals.reshape(-1, width)
    own = lax.psum_scatter(totals, "col", scatter_dimension=0, tiled=True)
    pre = own + bias
    output = jnp.maximum(pre, 0.0).astype(jnp.bfloat16)
    grad_own = jnp.where(pre > 0, cotangent.astype(jnp.float32), 0.0).astype(jnp.bfloat16)
    grad_panel = lax.all_gather(grad_own, "col", axis=0, tiled=True)
    grad_blocks = grad_panel.reshape(-1, 128, width)

    def backward_step(i, acc):
        start = i * batch
        dense = lax.dynamic_slice_in_dim(stored, start, batch, 0)
        rows_here = lax.dynamic_slice_in_dim(brow, start, batch, 0)
        cols_here = lax.dynamic_slice_in_dim(bcol, start, batch, 0)
        product = jnp.einsum(
            "bij,bif->bjf", dense, grad_blocks[rows_here], preferred_element_type=jnp.float32
        )
        select = (cols_here[:, None] == col_ids).astype(jnp.float32)
        added = jnp.einsum(
            "bc,bjf->cjf",
            select,
            product,
            precision=lax.Precision.HIGHEST,
            preferred_element_type=jnp.float32,
        )
        return acc + added

    acc0 = jnp.zeros((col_blocks, 128, width), jnp.float32)
    acc = lax.fori_loop(0, turns, backward_step, acc0)
    grad_proj = lax.psum_scatter(
        acc.reshape(-1, width), "row", scatter_dimension=0, tiled=True
    ).astype(jnp.bfloat16)
    grad_features = lax.dot_general(
        grad_proj, weight, (((1,), (1,)), ((), ())), preferred_element_type=jnp.float32
    ).astype(jnp.bfloat16)
    local_weight = lax.dot_general(
        features, grad_proj, (((0,), (0,)), ((), ())), preferred_element_type=jnp.float32
    )
    local_bias = jnp.sum(grad_own.astype(jnp.float32), axis=0)
    total_weight, total_bias = lax.psum((local_weight, local_bias), ("row", "col"))
    scale = (node_dev * n_row * n_col) ** (-0.5)
    return (output, grad_features, total_weight * scale, total_bias * scale)


def solution(mesh):
    return jax.shard_map(
        shards,
        mesh=mesh,
        in_specs=(
            P(("row", "col"), None),
            P(),
            P(),
            P(("row", "col"), None),
            P("row", "col"),
            P("row", "col", None),
            P("row", "col", None),
            P("row", "col", None, None),
            P("row", "col", None, None),
        ),
        out_specs=(P(("row", "col"), None), P(("row", "col"), None), P(), P()),
        check_vma=False,
    )
```

profile of v0, /device:TPU:1, one launch (start us, length us, event | category | flops | bytes accessed | tf_op | source)
XLA Modules:
  0.0 1005.6 jit_solution(10887614581579675863)
XLA Ops:
  8.1 1.6 convolution_convert_fusion.1
  10.4 34.3 %all-gather.3.cloned.1.call-done = bf16[4096,128]{1,0:T(8,128)(2,1)} async-done(((bf16[512,128]{1,0:T(8,128)(2,1)}), bf16[4096,128]{1,0:T(8,128)(2,1)}) %all-gather.3.cloned.1.call-update) | async-done | bytes 1048592 | tf_op jit(solution)/shard_map/all_gather | solution.py:36
  44.7 6.3 broadcast_in_dim.84
  51.0 4.3 broadcast_in_dim.85
  55.3 173.9 %while.29 = (s32[]{:T(128)}, bf16[512,128,128]{2,1,0:T(8,128)(2,1)}, f32[128,128,128]{2,0,1:T(8,128)}, s32[]{:T(128)}, s32[512,128]{1,0:T(8,128)}, /*index=5*/s3...) while((s32[]{:T(128)}, ...), condition=%wide.region_1.2_spmd.clone.clone, body=%wide.region_0.1_spmd.clone.clone.sunk | while | flops 2154005760 | bytes 38017104 | solution.py:69
  58.3 3.6 constant_dynamic-update-slice_fusion.2
  62.9 2.3 fusion.69
  65.3 11.7 %fusion.70 = f32[128,128,128]{2,0,1:T(8,128)} fusion(f32[128,128,128]{2,0,1:T(8,128)} %get-tuple-element.493, f32[64,128,128]{2,1,0:T(8,128)S(1)} %fusion.69, s32[64]{0:T(128)S(1)} %dynamic_slice.84), kind=kOutput, calls=%fused_computation.22.clone.1 | convolution fusion | flops 1612718080 | bytes 20971776 | tf_op jit(solution)/shard_map/while/body/br,bif->rif/dot_general | solution.py:58
  80.0 3.7 constant_dynamic-update-slice_fusion.2
  84.7 2.3 fusion.69
  87.1 11.7 %fusion.70 = f32[128,128,128]{2,0,1:T(8,128)} fusion(f32[128,128,128]{2,0,1:T(8,128)} %get-tuple-element.493, f32[64,128,128]{2,1,0:T(8,128)S(1)} %fusion.69, s32[64]{0:T(128)S(1)} %dynamic_slice.84), kind=kOutput, calls=%fused_computation.22.clone.1 | convolution fusion | flops 1612718080 | bytes 20971776 | tf_op jit(solution)/shard_map/while/body/br,bif->rif/dot_general | solution.py:58
  101.8 3.7 constant_dynamic-update-slice_fusion.2
  106.5 2.3 fusion.69
  108.9 11.7 %fusion.70 = f32[128,128,128]{2,0,1:T(8,128)} fusion(f32[128,128,128]{2,0,1:T(8,128)} %get-tuple-element.493, f32[64,128,128]{2,1,0:T(8,128)S(1)} %fusion.69, s32[64]{0:T(128)S(1)} %dynamic_slice.84), kind=kOutput, calls=%fused_computation.22.clone.1 | convolution fusion | flops 1612718080 | bytes 20971776 | tf_op jit(solution)/shard_map/while/body/br,bif->rif/dot_general | solution.py:58
  123.6 3.6 constant_dynamic-update-slice_fusion.2
  128.2 2.3 fusion.69
  130.6 11.7 %fusion.70 = f32[128,128,128]{2,0,1:T(8,128)} fusion(f32[128,128,128]{2,0,1:T(8,128)} %get-tuple-element.493, f32[64,128,128]{2,1,0:T(8,128)S(1)} %fusion.69, s32[64]{0:T(128)S(1)} %dynamic_slice.84), kind=kOutput, calls=%fused_computation.22.clone.1 | convolution fusion | flops 1612718080 | bytes 20971776 | tf_op jit(solution)/shard_map/while/body/br,bif->rif/dot_general | solution.py:58
  145.3 3.7 constant_dynamic-update-slice_fusion.2
  150.1 2.3 fusion.69
  152.4 11.7 %fusion.70 = f32[128,128,128]{2,0,1:T(8,128)} fusion(f32[128,128,128]{2,0,1:T(8,128)} %get-tuple-element.493, f32[64,128,128]{2,1,0:T(8,128)S(1)} %fusion.69, s32[64]{0:T(128)S(1)} %dynamic_slice.84), kind=kOutput, calls=%fused_computation.22.clone.1 | convolution fusion | flops 1612718080 | bytes 20971776 | tf_op jit(solution)/shard_map/while/body/br,bif->rif/dot_general | solution.py:58
  167.1 3.6 constant_dynamic-update-slice_fusion.2
  171.7 2.3 fusion.69
  174.1 11.7 %fusion.70 = f32[128,128,128]{2,0,1:T(8,128)} fusion(f32[128,128,128]{2,0,1:T(8,128)} %get-tuple-element.493, f32[64,128,128]{2,1,0:T(8,128)S(1)} %fusion.69, s32[64]{0:T(128)S(1)} %dynamic_slice.84), kind=kOutput, calls=%fused_computation.22.clone.1 | convolution fusion | flops 1612718080 | bytes 20971776 | tf_op jit(solution)/shard_map/while/body/br,bif->rif/dot_general | solution.py:58
  188.8 3.5 constant_dynamic-update-slice_fusion.2
  193.4 2.3 fusion.69
  195.8 11.7 %fusion.70 = f32[128,128,128]{2,0,1:T(8,128)} fusion(f32[128,128,128]{2,0,1:T(8,128)} %get-tuple-element.493, f32[64,128,128]{2,1,0:T(8,128)S(1)} %fusion.69, s32[64]{0:T(128)S(1)} %dynamic_slice.84), kind=kOutput, calls=%fused_computation.22.clone.1 | convolution fusion | flops 1612718080 | bytes 20971776 | tf_op jit(solution)/shard_map/while/body/br,bif->rif/dot_general | solution.py:58
  210.5 3.6 constant_dynamic-update-slice_fusion.2
  215.1 2.3 fusion.69
  217.5 11.7 %fusion.70 = f32[128,128,128]{2,0,1:T(8,128)} fusion(f32[128,128,128]{2,0,1:T(8,128)} %get-tuple-element.493, f32[64,128,128]{2,1,0:T(8,128)S(1)} %fusion.69, s32[64]{0:T(128)S(1)} %dynamic_slice.84), kind=kOutput, calls=%fused_computation.22.clone.1 | convolution fusion | flops 1612718080 | bytes 20971776 | tf_op jit(solution)/shard_map/while/body/br,bif->rif/dot_general | solution.py:58
  229.2 11.5 %copy.17 = f32[128,128,128]{2,1,0:T(8,128)} copy(f32[128,128,128]{2,0,1:T(8,128)} %get-tuple-element.240) | data formatting | bytes 16777216 | tf_op jit(solution)/shard_map/while | solution.py:69
  240.7 155.5 %reduce-scatter.3.cloned.1.call-done = f32[512,128]{1,0:T(8,128)} async-done(((f32[16384,128]{1,0:T(8,128)}), f32[512,128]{1,0:T(8,128)}) %reduce-scatter.3.cloned.1.call-update) | async-done | bytes 262160 | tf_op jit(solution)/shard_map/reduce_scatter | solution.py:71
  396.3 1.7 convert_reduce_fusion
  398.1 160.6 %all-gather.5.cloned.1.call-done = bf16[16384,128]{1,0:T(8,128)(2,1)} async-done(((bf16[512,128]{1,0:T(8,128)(2,1)}), bf16[16384,128]{1,0:T(8,128)(2,1)}) %all-gather.5.cloned.1.call-update) | async-done | bytes 4194320 | tf_op jit(solution)/shard_map/all_gather | solution.py:75
  558.7 1.6 broadcast_in_dim.86
  560.3 101.9 %while.28 = (s32[]{:T(128)}, f32[32,128,128]{2,0,1:T(8,128)}, s32[]{:T(128)}, s32[512]{0:T(512)S(1)}, bf16[512,128,128]{2,1,0:T(8,128)(2,1)}, /*index=5*/s32[512...) while((s32[]{:T(128)}, f32[32,128,128]{2,0,1:T(8,128)}, ...), condition=%wide.region_4.5_spmd.clone, body=%wide.region_3.4_spmd.clone.sunk | while | flops 671616192 | bytes 20977576 | solution.py:97
  560.4 3.1 gather_fusion
  563.5 2.5 fusion.62
  566.1 7.0 fusion.63
  573.1 3.1 gather_fusion
  576.3 2.5 fusion.62
  578.8 7.0 fusion.63
  585.9 3.1 gather_fusion
  589.0 2.5 fusion.62
  591.5 7.0 fusion.63
  598.6 3.1 gather_fusion
  601.7 2.5 fusion.62
  604.3 7.0 fusion.63
  611.3 3.1 gather_fusion
  614.5 2.5 fusion.62
  617.0 7.0 fusion.63
  624.1 3.1 gather_fusion
  627.2 2.5 fusion.62
  629.8 7.0 fusion.63
  636.8 3.1 gather_fusion
  640.0 2.5 fusion.62
  642.5 7.0 fusion.63
  649.6 3.1 gather_fusion
  652.7 2.5 fusion.62
  655.2 7.0 fusion.63
  662.2 4.1 copy.18
  666.4 93.1 %psum.15 = f32[128]{0:T(128)S(1)} all-reduce(f32[128]{0:T(128)S(1)} %get-tuple-element.358), channel_id=1, replica_groups=mesh['row'=8,'col'=32] {'row','col'}, use_global_device_ids=true, to_apply=%region_8.9 | all-reduce | flops 128 | bytes 1024 | tf_op jit(solution)/shard_map/psum | solution.py:108
  760.1 1.8 convolution_bitcast_fusion
  761.9 1.8 convolution_convert_fusion
  763.7 233.7 %all-reduce.2.cloned.1.call-done = f32[128,128]{0,1:T(8,128)} async-done(((f32[128,128]{0,1:T(8,128)}), f32[128,128]{0,1:T(8,128)}) %all-reduce.2.cloned.1.call-update) | async-done | bytes 65552 | tf_op jit(solution)/shard_map/psum | solution.py:108
  (116 shorter events, 37.6 us)
Async XLA Ops:
  7.2 0.9 copy-start
  7.2 37.5 %all-gather.3.cloned.1.call-start = ((), (), s32[]{:S(2)}) async-start(), calls=%async_computation.2 | async-start | bytes 1179648 | tf_op jit(solution)/shard_map/all_gather | solution.py:36
  9.7 386.6 %reduce-scatter.3.cloned.1.call-start = ((), (), s32[]{:S(2)}) async-start(), calls=%async_computation.3 | async-start | bytes 8650752 | tf_op jit(solution)/shard_map/reduce_scatter | solution.py:71
  51.0 4.3 copy-start.1
  51.0 4.3 copy-start.5
  51.0 4.3 copy-start.6
  240.7 155.6 %copy-start.2 = (bf16[512,128]{1,0:T(8,128)(2,1)S(1)}, bf16[512,128]{1,0:T(8,128)(2,1)}, u32[]{:S(2)}) copy-start(bf16[512,128]{1,0:T(8,128)(2,1)} %param.16) | copy-start | bytes 393220
  240.7 155.6 %copy-start.4 = (f32[128]{0:T(128)S(1)}, f32[128]{0:T(128)}, u32[]{:S(2)}) copy-start(f32[128]{0:T(128)} %param.15) | copy-start | bytes 1540
  240.7 318.0 %all-gather.5.cloned.1.call-start = ((), (), s32[]{:S(2)}) async-start(), calls=%async_computation.4 | async-start | bytes 4325376 | tf_op jit(solution)/shard_map/all_gather | solution.py:75
  398.0 362.1 %reduce-scatter.5.cloned.1.call-start = ((), (), s32[]{:S(2)}) async-start(), calls=%async_computation.5 | async-start | bytes 2359296 | tf_op jit(solution)/shard_map/reduce_scatter | solution.py:98
  662.2 99.7 %copy-start.3 = (bf16[128,128]{1,0:T(8,128)(2,1)S(1)}, bf16[128,128]{1,0:T(8,128)(2,1)}, u32[]{:S(2)}) copy-start(bf16[128,128]{1,0:T(8,128)(2,1)} %param.14) | copy-start | bytes 98308
  666.4 331.1 %all-reduce.2.cloned.1.call-start = ((), (), s32[]{:S(2)}) async-start(), calls=%async_computation.6 | async-start | bytes 131072 | tf_op jit(solution)/shard_map/psum | solution.py:108
Sparse Core Ops, SparseCore 0:
  10.4 34.2 all-gather.2
  240.8 155.4 reduce-scatter.2
  398.6 160.0 all-gather.4
  666.5 58.0 reduce-scatter.4
  762.0 235.3 all-reduce.1
where the time goes:
time: 1010 us
  waiting for transfers between devices  584 us (58%)
  matrix products  221 us (22%)
  blocking collectives  93.1 us (9%)
  local copies, waits for them, and re-layouts  63.3 us (6%)
  other arithmetic  28.6 us (3%)
  between operations  14.5 us (1%)
    psum x1, waiting for transfers between devices, shards(): lax.psum((local_weight, local_bias), ('row', 'col'))  234 us
    all_gather x1, waiting for transfers between devices, shards(): grad_panel = lax.all_gather(grad_own, 'col', axis=0, tiled=True)  161 us
    reduce_scatter x1, waiting for transfers between devices, shards(): own = lax.psum_scatter(totals, 'col', scatter_dimension=0, tiled=True)  156 us
    dot_general x8, matrix products, forward_step(): jnp.einsum('br,bif->rif', select, product, precision=lax.Precision.HIGHES...  93.5 us
    psum x1, blocking collectives, shards(): lax.psum((local_weight, local_bias), ('row', 'col'))  93.1 us
    dot_general x8, matrix products, backward_step(): jnp.einsum('bc,bjf->cjf', select, product, precision=lax.Precision.HIGHES...  55.8 us
    all_gather x1, waiting for transfers between devices, shards(): lax.all_gather(projected, 'row', axis=0, tiled=True).reshape(-1, 128, width)  34.3 us
    dot_general x8, matrix products, forward_step(): jnp.einsum('bei,bej->bij', left, right, preferred_element_type=jnp.float32)  28.9 us
  transfers between devices with their start and end apart: 5, of which 4 were waited for; matrix products, arithmetic and copies ran while one was open for 0% of the time, Pallas kernels for 0%

commit v1 on v0

--- a/solution.py
+++ b/solution.py
@@ -105,7 +105,7 @@
         features, grad_proj, (((0,), (0,)), ((), ())), preferred_element_type=jnp.float32
     )
     local_bias = jnp.sum(grad_own.astype(jnp.float32), axis=0)
-    total_weight, total_bias = lax.psum((local_weight, local_bias), ("row", "col"))
+    total_weight, total_bias = lax.psum(lax.psum((local_weight, local_bias), "row"), "col")
     scale = (node_dev * n_row * n_col) ** (-0.5)
     return (output, grad_features, total_weight * scale, total_bias * scale)
 

time: 1010 us -> 1130 us (1.12)
  waiting for transfers between devices: 584 us -> 692 us
    psum x1 -> x2, waiting for transfers between devices: 234 us -> 342 us  [the longest x1 261 us: shards(): lax.psum(lax.psum((local_weight, local_bias), 'row'), 'col')]
    psum x1 -> x2, blocking collectives: 93.1 us -> 97.9 us  [the longest x1 65.8 us: shards(): lax.psum(lax.psum((local_weight, local_bias), 'row'), 'col')]
  transfers between devices with their start and end apart: 5 -> 6, of which waited for: 4 -> 5; matrix products, arithmetic and copies ran while one was open for 0% -> 0% of each run, Pallas kernels for 0% -> 0%
where the time goes in v1:
time: 1130 us; the launch traced here: 1120 us
  waiting for transfers between devices  692 us (61%)
  matrix products  221 us (20%)
  blocking collectives  97.9 us (9%)
  local copies, waits for them, and re-layouts  63.3 us (6%)
  other arithmetic  28.6 us (3%)
  between operations  14.8 us (1%)
    psum x1, waiting for transfers between devices, shards(): lax.psum(lax.psum((local_weight, local_bias), 'row'), 'col')  261 us
    all_gather x1, waiting for transfers between devices, shards(): grad_panel = lax.all_gather(grad_own, 'col', axis=0, tiled=True)  159 us
    reduce_scatter x1, waiting for transfers between devices, shards(): own = lax.psum_scatter(totals, 'col', scatter_dimension=0, tiled=True)  157 us
    dot_general x8, matrix products, forward_step(): jnp.einsum('br,bif->rif', select, product, precision=lax.Precision.HIGHES...  93.5 us
    psum x1, waiting for transfers between devices, shards(): lax.psum((local_weight, local_bias), 'row')  80.3 us
    psum x1, blocking collectives, shards(): lax.psum(lax.psum((local_weight, local_bias), 'row'), 'col')  65.8 us
    dot_general x8, matrix products, backward_step(): jnp.einsum('bc,bjf->cjf', select, product, precision=lax.Precision.HIGHES...  55.7 us
    all_gather x1, waiting for transfers between devices, shards(): lax.all_gather(projected, 'row', axis=0, tiled=True).reshape(-1, 128, width)  34.3 us
  transfers between devices with their start and end apart: 6, of which 5 were waited for; matrix products, arithmetic and copies ran while one was open for 0% of the time, Pallas kernels for 0%

profile of v1, /device:TPU:1, one launch (start us, length us, event | category | flops | bytes accessed | tf_op | source)
XLA Modules:
  0.0 1118.5 jit_solution(11262162803905647158)
XLA Ops:
  10.4 34.3 %all-gather.3.cloned.1.call-done = bf16[4096,128]{1,0:T(8,128)(2,1)} async-done(((bf16[512,128]{1,0:T(8,128)(2,1)}), bf16[4096,128]{1,0:T(8,128)(2,1)}) %all-gather.3.cloned.1.call-update) | async-done | bytes 1048592 | tf_op jit(solution)/shard_map/all_gather | solution.py:36
  44.7 6.3 broadcast_in_dim.84
  51.0 4.3 broadcast_in_dim.85
  55.3 174.0 %while.29 = (s32[]{:T(128)}, bf16[512,128,128]{2,1,0:T(8,128)(2,1)}, f32[128,128,128]{2,0,1:T(8,128)}, s32[]{:T(128)}, s32[512,128]{1,0:T(8,128)}, /*index=5*/s3...) while((s32[]{:T(128)}, ...), condition=%wide.region_1.2_spmd.clone.clone, body=%wide.region_0.1_spmd.clone.clone.sunk | while | flops 2154005760 | bytes 38017104 | solution.py:69
  58.4 3.6 constant_dynamic-update-slice_fusion.2
  63.0 2.3 fusion.69
  65.3 11.7 %fusion.70 = f32[128,128,128]{2,0,1:T(8,128)} fusion(f32[128,128,128]{2,0,1:T(8,128)} %get-tuple-element.493, f32[64,128,128]{2,1,0:T(8,128)S(1)} %fusion.69, s32[64]{0:T(128)S(1)} %dynamic_slice.84), kind=kOutput, calls=%fused_computation.22.clone.1 | convolution fusion | flops 1612718080 | bytes 20971776 | tf_op jit(solution)/shard_map/while/body/br,bif->rif/dot_general | solution.py:58
  80.1 3.6 constant_dynamic-update-slice_fusion.2
  84.8 2.3 fusion.69
  87.1 11.7 %fusion.70 = f32[128,128,128]{2,0,1:T(8,128)} fusion(f32[128,128,128]{2,0,1:T(8,128)} %get-tuple-element.493, f32[64,128,128]{2,1,0:T(8,128)S(1)} %fusion.69, s32[64]{0:T(128)S(1)} %dynamic_slice.84), kind=kOutput, calls=%fused_computation.22.clone.1 | convolution fusion | flops 1612718080 | bytes 20971776 | tf_op jit(solution)/shard_map/while/body/br,bif->rif/dot_general | solution.py:58
  101.8 3.7 constant_dynamic-update-slice_fusion.2
  106.5 2.3 fusion.69
  108.9 11.7 %fusion.70 = f32[128,128,128]{2,0,1:T(8,128)} fusion(f32[128,128,128]{2,0,1:T(8,128)} %get-tuple-element.493, f32[64,128,128]{2,1,0:T(8,128)S(1)} %fusion.69, s32[64]{0:T(128)S(1)} %dynamic_slice.84), kind=kOutput, calls=%fused_computation.22.clone.1 | convolution fusion | flops 1612718080 | bytes 20971776 | tf_op jit(solution)/shard_map/while/body/br,bif->rif/dot_general | solution.py:58
  123.6 3.6 constant_dynamic-update-slice_fusion.2
  128.3 2.3 fusion.69
  130.6 11.7 %fusion.70 = f32[128,128,128]{2,0,1:T(8,128)} fusion(f32[128,128,128]{2,0,1:T(8,128)} %get-tuple-element.493, f32[64,128,128]{2,1,0:T(8,128)S(1)} %fusion.69, s32[64]{0:T(128)S(1)} %dynamic_slice.84), kind=kOutput, calls=%fused_computation.22.clone.1 | convolution fusion | flops 1612718080 | bytes 20971776 | tf_op jit(solution)/shard_map/while/body/br,bif->rif/dot_general | solution.py:58
  145.3 3.7 constant_dynamic-update-slice_fusion.2
  150.1 2.3 fusion.69
  152.5 11.7 %fusion.70 = f32[128,128,128]{2,0,1:T(8,128)} fusion(f32[128,128,128]{2,0,1:T(8,128)} %get-tuple-element.493, f32[64,128,128]{2,1,0:T(8,128)S(1)} %fusion.69, s32[64]{0:T(128)S(1)} %dynamic_slice.84), kind=kOutput, calls=%fused_computation.22.clone.1 | convolution fusion | flops 1612718080 | bytes 20971776 | tf_op jit(solution)/shard_map/while/body/br,bif->rif/dot_general | solution.py:58
  167.2 3.6 constant_dynamic-update-slice_fusion.2
  171.8 2.3 fusion.69
  174.2 11.7 %fusion.70 = f32[128,128,128]{2,0,1:T(8,128)} fusion(f32[128,128,128]{2,0,1:T(8,128)} %get-tuple-element.493, f32[64,128,128]{2,1,0:T(8,128)S(1)} %fusion.69, s32[64]{0:T(128)S(1)} %dynamic_slice.84), kind=kOutput, calls=%fused_computation.22.clone.1 | convolution fusion | flops 1612718080 | bytes 20971776 | tf_op jit(solution)/shard_map/while/body/br,bif->rif/dot_general | solution.py:58
  188.9 3.6 constant_dynamic-update-slice_fusion.2
  193.5 2.3 fusion.69
  195.9 11.7 %fusion.70 = f32[128,128,128]{2,0,1:T(8,128)} fusion(f32[128,128,128]{2,0,1:T(8,128)} %get-tuple-element.493, f32[64,128,128]{2,1,0:T(8,128)S(1)} %fusion.69, s32[64]{0:T(128)S(1)} %dynamic_slice.84), kind=kOutput, calls=%fused_computation.22.clone.1 | convolution fusion | flops 1612718080 | bytes 20971776 | tf_op jit(solution)/shard_map/while/body/br,bif->rif/dot_general | solution.py:58
  210.6 3.6 constant_dynamic-update-slice_fusion.2
  215.2 2.3 fusion.69
  217.6 11.7 %fusion.70 = f32[128,128,128]{2,0,1:T(8,128)} fusion(f32[128,128,128]{2,0,1:T(8,128)} %get-tuple-element.493, f32[64,128,128]{2,1,0:T(8,128)S(1)} %fusion.69, s32[64]{0:T(128)S(1)} %dynamic_slice.84), kind=kOutput, calls=%fused_computation.22.clone.1 | convolution fusion | flops 1612718080 | bytes 20971776 | tf_op jit(solution)/shard_map/while/body/br,bif->rif/dot_general | solution.py:58
  229.3 11.5 %copy.17 = f32[128,128,128]{2,1,0:T(8,128)} copy(f32[128,128,128]{2,0,1:T(8,128)} %get-tuple-element.240) | data formatting | bytes 16777216 | tf_op jit(solution)/shard_map/while | solution.py:69
  240.8 156.7 %reduce-scatter.3.cloned.1.call-done = f32[512,128]{1,0:T(8,128)} async-done(((f32[16384,128]{1,0:T(8,128)}), f32[512,128]{1,0:T(8,128)}) %reduce-scatter.3.cloned.1.call-update) | async-done | bytes 262160 | tf_op jit(solution)/shard_map/reduce_scatter | solution.py:71
  397.6 1.7 convert_reduce_fusion
  399.4 159.1 %all-gather.5.cloned.1.call-done = bf16[16384,128]{1,0:T(8,128)(2,1)} async-done(((bf16[512,128]{1,0:T(8,128)(2,1)}), bf16[16384,128]{1,0:T(8,128)(2,1)}) %all-gather.5.cloned.1.call-update) | async-done | bytes 4194320 | tf_op jit(solution)/shard_map/all_gather | solution.py:75
  560.1 101.9 %while.28 = (s32[]{:T(128)}, f32[32,128,128]{2,0,1:T(8,128)}, s32[]{:T(128)}, s32[512]{0:T(512)S(1)}, bf16[512,128,128]{2,1,0:T(8,128)(2,1)}, /*index=5*/s32[512...) while((s32[]{:T(128)}, f32[32,128,128]{2,0,1:T(8,128)}, ...), condition=%wide.region_4.5_spmd.clone, body=%wide.region_3.4_spmd.clone.sunk | while | flops 671616192 | bytes 20977576 | solution.py:97
  560.1 3.1 gather_fusion
  563.3 2.5 fusion.62
  565.8 7.0 fusion.63
  572.9 3.1 gather_fusion
  576.0 2.5 fusion.62
  578.6 7.0 fusion.63
  585.6 3.1 gather_fusion
  588.8 2.5 fusion.62
  591.3 7.0 fusion.63
  598.4 3.1 gather_fusion
  601.5 2.5 fusion.62
  604.0 7.0 fusion.63
  611.1 3.1 gather_fusion
  614.2 2.5 fusion.62
  616.8 7.0 fusion.63
  623.8 3.1 gather_fusion
  627.0 2.5 fusion.62
  629.5 7.0 fusion.63
  636.6 3.1 gather_fusion
  639.7 2.5 fusion.62
  642.3 7.0 fusion.63
  649.3 3.1 gather_fusion
  652.5 2.5 fusion.62
  655.0 7.0 fusion.63
  662.0 4.2 copy.18
  666.2 32.2 %psum.30 = f32[128]{0:T(128)S(1)} all-reduce(f32[128]{0:T(128)S(1)} %get-tuple-element.358), channel_id=1, replica_groups=mesh['row'=8,'col'=32] {'row'}, use_global_device_ids=true, to_apply=%region_9.10 | all-reduce | flops 128 | bytes 1024 | tf_op jit(solution)/shard_map/psum | solution.py:108
  698.3 65.8 %psum.31 = f32[128]{0:T(128)S(1)} all-reduce(f32[128]{0:T(128)S(1)} %psum.30), channel_id=1, replica_groups=mesh['row'=8,'col'=32] {'col'}, use_global_device_ids=true, to_apply=%region_10.11 | all-reduce | flops 128 | bytes 1024 | tf_op jit(solution)/shard_map/psum | solution.py:108
  764.1 1.8 convolution_bitcast_fusion
  766.5 80.3 %all-reduce.3.cloned.1.call-done = f32[128,128]{0,1:T(8,128)} async-done(((f32[128,128]{0,1:T(8,128)}), f32[128,128]{0,1:T(8,128)}) %all-reduce.3.cloned.1.call-update) | async-done | bytes 65552 | tf_op jit(solution)/shard_map/psum | solution.py:108
  846.8 1.8 convolution_convert_fusion
  848.6 261.5 %all-reduce.5.cloned.1.call-done = f32[128,128]{0,1:T(8,128)} async-done(((f32[128,128]{0,1:T(8,128)}), f32[128,128]{0,1:T(8,128)}) %all-reduce.5.cloned.1.call-update) | async-done | bytes 65552 | tf_op jit(solution)/shard_map/psum | solution.py:108
  (120 shorter events, 40.8 us)
Async XLA Ops:
  7.2 0.9 copy-start
  7.2 37.5 %all-gather.3.cloned.1.call-start = ((), (), s32[]{:S(2)}) async-start(), calls=%async_computation.2 | async-start | bytes 1179648 | tf_op jit(solution)/shard_map/all_gather | solution.py:36
  9.7 387.9 %reduce-scatter.3.cloned.1.call-start = ((), (), s32[]{:S(2)}) async-start(), calls=%async_computation.3 | async-start | bytes 8650752 | tf_op jit(solution)/shard_map/reduce_scatter | solution.py:71
  51.0 4.3 copy-start.1
  51.0 4.3 copy-start.5
  51.0 4.3 copy-start.6
  240.7 156.8 %copy-start.2 = (bf16[512,128]{1,0:T(8,128)(2,1)S(1)}, bf16[512,128]{1,0:T(8,128)(2,1)}, u32[]{:S(2)}) copy-start(bf16[512,128]{1,0:T(8,128)(2,1)} %param.16) | copy-start | bytes 393220
  240.7 156.8 %copy-start.4 = (f32[128]{0:T(128)S(1)}, f32[128]{0:T(128)}, u32[]{:S(2)}) copy-start(f32[128]{0:T(128)} %param.15) | copy-start | bytes 1540
  240.8 317.7 %all-gather.5.cloned.1.call-start = ((), (), s32[]{:S(2)}) async-start(), calls=%async_computation.4 | async-start | bytes 4325376 | tf_op jit(solution)/shard_map/all_gather | solution.py:75
  399.3 364.8 %reduce-scatter.5.cloned.1.call-start = ((), (), s32[]{:S(2)}) async-start(), calls=%async_computation.5 | async-start | bytes 2359296 | tf_op jit(solution)/shard_map/reduce_scatter | solution.py:98
  662.0 184.8 %copy-start.3 = (bf16[128,128]{1,0:T(8,128)(2,1)S(1)}, bf16[128,128]{1,0:T(8,128)(2,1)}, u32[]{:S(2)}) copy-start(bf16[128,128]{1,0:T(8,128)(2,1)} %param.14) | copy-start | bytes 98308
  666.1 180.6 %all-reduce.3.cloned.1.call-start = ((), (), s32[]{:S(2)}) async-start(), calls=%async_computation.6 | async-start | bytes 131072 | tf_op jit(solution)/shard_map/psum | solution.py:108
  766.0 344.1 %all-reduce.5.cloned.1.call-start = ((), (), s32[]{:S(2)}) async-start(), calls=%async_computation.7 | async-start | bytes 131072 | tf_op jit(solution)/shard_map/psum | solution.py:108
Sparse Core Ops, SparseCore 0:
  10.4 34.2 all-gather.2
  240.9 156.6 reduce-scatter.2
  399.9 158.4 all-gather.4
  666.3 57.6 reduce-scatter.4
  766.1 80.6 all-reduce.2
  849.4 260.6 all-reduce.4
